TPU v7x, 32 devices: a whole 2x2x4 slice. The times are simulated.
32 devices in a mesh: grp: 2 (over y), seq: 8 (over z, x), mdl: 2 (over core).
Axes of the slice: x: 2, y: 2, z: 4, core: 2. Of those that a mesh axis runs over, the one named last changes fastest.
Arguments:
- signal: bfloat16 [2048, 2048], P(('grp', 'seq'), 'mdl'), parts along dimension 0, may hold values from -6 to 6
- gate_first: bfloat16 [2048, 2048], P(('grp', 'seq'), 'mdl'), parts along dimension 0, may hold values from -6 to 6
- gate_second: bfloat16 [2048, 2048], P(('grp', 'seq'), 'mdl'), parts along dimension 0, may hold values from -6 to 6
- spectrum_first: bfloat16 [2, 16, 128, 2048], P(None, 'seq', None, 'mdl'), may hold values from -8 to 8
- spectrum_second: bfloat16 [2, 16, 128, 2048], P(None, 'seq', None, 'mdl'), may hold values from -8 to 8
- skip_first: float32 [2048], P('mdl'), may hold values from 0.5 to 1.5
- skip_second: float32 [2048], P('mdl'), may hold values from 0.5 to 1.5
- out_weight: bfloat16 [2048, 2048], P('seq', 'mdl'), may hold values from -0.125 to 0.125
Outputs:
- block_out: bfloat16 [2048, 2048], P(('grp', 'seq'), 'mdl'), parts along dimension 0
There are 2 independent parts, one for each index of `grp`. A program takes and returns all parts, laid end to end along the dimension named above; an argument that names none is the same for every part. Nothing has to cross between parts.
All inputs are finite; a program needn't handle non-finite values.
Results may differ from a plain program's by a relative error of at most 0.0057.
Values may be sent and summed in bfloat16 or wider, within the bound.
A program may use at most 64 MiB of HBM per device.

v0:
```python
import math
import jax
import jax.numpy as jnp
from jax import lax
from jax.sharding import PartitionSpec as P


def angle_grid(first, second, modulus):
    product = first[:, None] * second[None, :] % modulus
    angles = product.astype(jnp.float32) * (2.0 * math.pi / modulus)
    return (jnp.cos(angles), jnp.sin(angles))


def mixing(form, left, right):
    return jnp.einsum(form, left, right, precision=lax.Precision.HIGHEST)


def complex_mix(form, real_table, imag_table, values_re, values_im):
    first_term = mixing(form, real_table, values_re + values_im)
    second_term = mixing(form, real_table + imag_table, values_im)
    third_term = mixing(form, imag_table - real_table, values_re)
    return (first_term - second_term, first_term + third_term)


def channel_filter(field, spectrum):
    coarse = spectrum.shape[1]
    span = spectrum.shape[2]
    count = coarse // 2
    cols = field.shape[1]
    length = coarse * span
    pencil = field.reshape(count, span, cols)
    coarse_ids = jnp.arange(coarse, dtype=jnp.int32)
    cos_a, sin_a = angle_grid(coarse_ids, jnp.arange(count, dtype=jnp.int32), coarse)
    part_re = mixing("ka,amc->kmc", cos_a, pencil)
    part_im = -mixing("ka,amc->kmc", sin_a, pencil)
    fine_ids = jnp.arange(span, dtype=jnp.int32)
    cos_t, sin_t = angle_grid(coarse_ids, fine_ids, length)
    cos_t = cos_t[:, :, None]
    sin_t = sin_t[:, :, None]
    turned_re = part_re * cos_t + part_im * sin_t
    turned_im = part_im * cos_t - part_re * sin_t
    cos_s, sin_s = angle_grid(fine_ids, fine_ids, span)
    full_re, full_im = complex_mix("qm,kmc->kqc", cos_s, -sin_s, turned_re, turned_im)
    filt_re = spectrum[0].astype(jnp.float32)
    filt_im = spectrum[1].astype(jnp.float32)
    prod_re = filt_re * full_re - filt_im * full_im
    prod_im = filt_re * full_im + filt_im * full_re
    inner_re, inner_im = complex_mix("mq,kqc->kmc", cos_s, sin_s, prod_re, prod_im)
    back_re = inner_re * cos_t - inner_im * sin_t
    back_im = inner_im * cos_t + inner_re * sin_t
    result = mixing("ka,kmc->amc", cos_a, back_re) - mixing("ka,kmc->amc", sin_a, back_im)
    return (result / length).reshape(count * span, cols)


def shards(
    signal,
    gate_first,
    gate_second,
    spectrum_first,
    spectrum_second,
    skip_first,
    skip_second,
    out_weight,
):
    seq_index = lax.axis_index("seq")
    width = signal.shape[1]
    parts_seq = lax.axis_size("seq")
    cols = width // parts_seq
    col_sig, col_first, col_second = (
        lax.all_to_all(signal, "seq", split_axis=1, concat_axis=0, tiled=True),
        lax.all_to_all(gate_first, "seq", split_axis=1, concat_axis=0, tiled=True),
        lax.all_to_all(gate_second, "seq", split_axis=1, concat_axis=0, tiled=True),
    )
    spec_one, spec_two = (
        lax.all_to_all(spectrum_first, "seq", split_axis=3, concat_axis=1, tiled=True),
        lax.all_to_all(spectrum_second, "seq", split_axis=3, concat_axis=1, tiled=True),
    )
    skip_one = lax.dynamic_slice_in_dim(skip_first, seq_index * cols, cols, 0)
    skip_two = lax.dynamic_slice_in_dim(skip_second, seq_index * cols, cols, 0)
    values = col_sig.astype(jnp.float32)
    first_conv = channel_filter(values, spec_one) + skip_one * values
    first_out = (col_first.astype(jnp.float32) * first_conv).astype(jnp.bfloat16)
    first_vals = first_out.astype(jnp.float32)
    second_conv = channel_filter(first_vals, spec_two) + skip_two * first_vals
    mixed_cols = (col_second.astype(jnp.float32) * second_conv).astype(jnp.bfloat16)
    mixed = lax.all_to_all(mixed_cols, "seq", split_axis=0, concat_axis=1, tiled=True)
    features = lax.all_gather(mixed, "mdl", axis=1, tiled=True)
    total = jnp.dot(
        features,
        lax.all_gather(out_weight, "seq", axis=0, tiled=True),
        preferred_element_type=jnp.float32,
    )
    return total.astype(jnp.bfloat16)


def solution(mesh):
    placed = (
        P(("grp", "seq"), "mdl"),
        P(("grp", "seq"), "mdl"),
        P(("grp", "seq"), "mdl"),
        P(None, "seq", None, "mdl"),
        P(None, "seq", None, "mdl"),
        P("mdl"),
        P("mdl"),
        P("seq", "mdl"),
    )
    return jax.shard_map(
        shards, mesh=mesh, in_specs=placed, out_specs=P(("grp", "seq"), "mdl"), check_vma=False
    )
```

profile of v0, /device:TPU:0, one launch (start us, length us, event | category | flops | bytes accessed | tf_op | source)
XLA Modules:
  0.0 189.6 jit_solution(12314016013267601482)
XLA Ops:
  6.5 1.2 copy.80
  7.8 0.9 copy.81
  8.6 7.4 %all-to-all-start.4 = ((bf16[128,8,128]{2,0,1:T(8,128)(2,1)}), bf16[128,8,128]{2,0,1:T(8,128)(2,1)S(1)}, u32[]{:S(2)}, u32[]{:S(2)}) async-start(bf16[128,8,128]{2,0,1:T(8,128)(2,1)} %copy.81), calls=%async_computation.4 | async-start | bytes 524288 | tf_op jit(solution)/shard_map/all_to_all | solution.py:70
  16.0 3.7 %copy.78 = bf16[2,2,128,1024]{2,1,0,3:T(2,128)(2,1)} copy(bf16[2,2,128,1024]{3,2,1,0:T(8,128)(2,1)} %param.11) | data formatting | bytes 2097152 | tf_op args[3]
  19.7 5.2 %all-to-all-done.4 = bf16[128,8,128]{2,0,1:T(8,128)(2,1)S(1)} async-done(((bf16[128,8,128]{2,0,1:T(8,128)(2,1)}), bf16[128,8,128]{2,0,1:T(8,128)(2,1)S(1)}, u32[]{:S(2)}, u32[]{:S(2)}) %all-to-all-start.4) | async-done | bytes 262176 | tf_op jit(solution)/shard_map/all_to_all | solution.py:70
  24.9 3.6 %all-to-all-start.3 = ((bf16[2,2,128,1024]{2,1,0,3:T(2,128)(2,1)}), bf16[2,2,128,1024]{2,1,0,3:T(2,128)(2,1)S(1)}, u32[]{:S(2)}, u32[]{:S(2)}) async-start(bf16[2,2,128,1024]{2,1,0,3:T(2,128)(2,1)} %copy.78), calls=%async_computation.3 | async-start | bytes 2097152 | tf_op jit(solution)/shard_map/all_to_all | solution.py:75
  28.5 0.0 all-gather.2.cloned.1.call-start
  28.6 0.7 all-gather.2.cloned.1.call-update
  29.2 0.1 fusion.83
  29.3 0.1 copy.83
  29.4 0.1 copy.84
  29.5 0.0 copy-done.2
  29.5 0.2 copy.75
  29.7 0.9 copy.76
  30.6 0.0 copy-done.1
  30.6 2.0 %copy.73 = bf16[2,2,128,1024]{2,1,0,3:T(2,128)(2,1)} copy(bf16[2,2,128,1024]{3,2,1,0:T(8,128)(2,1)S(1)} %copy-done.1) | data formatting | bytes 2097152 | tf_op args[4]
  32.6 1.3 dynamic_slice.6
  33.9 1.3 dynamic_slice.7
  35.3 0.0 copy-done.3
  35.3 0.2 copy.70
  35.5 0.9 copy.71
  36.3 0.7 convolution_negate_fusion.1
  37.0 2.6 %fusion.179 = (f32[16,128,128]{2,0,1:T(8,128)S(1)}, f32[16,128,128]{2,0,1:T(8,128)S(1)}, f32[16,128,128]{2,0,1:T(8,128)}) fusion(f32[16,128]{0,1:T(8,128)S(1)} %copy.84, f32[16,128,128]{2,0,1:T(8,128)S(1)} %convolution_negate_fusion.1, f32[16,128]{0,1:T(8,128)S(1)} %copy.83, bf16[128,8,128]{2,0,1:T(8,128)(2,1)S(1)} %all-to-all-done.4), kind=kOutput, calls=%fused_computation.205 | convolution fusion | flops 27002624 | bytes 4472832 | tf_op jit(solution)/shard_map/ka,amc->kmc/dot_general | solution.py:15
  39.6 29.2 %all-to-all-done.3 = bf16[2,2,128,1024]{2,1,0,3:T(2,128)(2,1)S(1)} async-done(((bf16[2,2,128,1024]{2,1,0,3:T(2,128)(2,1)}), bf16[2,2,128,1024]{2,1,0,3:T(2,128)(2,1)S(1)}, u32[]{:S(2)}, u32[]{:S(2)}) %all-to-all-start.3) | async-done | bytes 1048608 | tf_op jit(solution)/shard_map/all_to_all | solution.py:75
  68.8 4.4 %all-to-all-start.1 = ((bf16[2,2,128,1024]{2,1,0,3:T(2,128)(2,1)}), bf16[2,2,128,1024]{2,1,0,3:T(2,128)(2,1)}, u32[]{:S(2)}, u32[]{:S(2)}) async-start(bf16[2,2,128,1024]{2,1,0,3:T(2,128)(2,1)} %copy.73), calls=%async_computation.1 | async-start | bytes 2097152 | tf_op jit(solution)/shard_map/all_to_all | solution.py:76
  73.3 2.1 %fusion.22 = f32[16,128,128]{2,1,0:T(8,128)S(1)} fusion(f32[16,128,128]{2,0,1:T(8,128)S(1)} %get-tuple-element.8), kind=kOutput, calls=%fused_computation.43 | convolution fusion | flops 402882560 | bytes 2097152 | tf_op jit(solution)/shard_map/qm,kmc->kqc/dot_general | solution.py:15
  75.4 0.0 copy-start
  75.4 2.2 %fusion.3 = f32[16,128,128]{1,2,0:T(8,128)S(1)} fusion(f32[16,128,128]{2,1,0:T(8,128)S(1)} %fusion.22, f32[16,128,128]{2,0,1:T(8,128)S(1)} %get-tuple-element.9), kind=kOutput, calls=%fused_computation.12 | convolution fusion | flops 403177472 | bytes 3145728 | tf_op jit(solution)/shard_map/qm,kmc->kqc/dot_general | solution.py:15
  77.6 0.2 copy.128
  77.8 0.1 fusion.181
  77.9 0.0 copy-done
  77.9 2.4 %fusion.13 = (f32[16,128,128]{1,2,0:T(8,128)S(1)}, f32[16,128,128]{1,2,0:T(8,128)S(1)}) fusion(f32[16,128,128]{1,2,0:T(8,128)S(1)} %fusion.3, bf16[1,8,2,128,128]{3,4,2,1,0:T(8,128)(2,1)S(1)} %get-tuple-element.22, bf16[1,8,2,128,128]{3,4,2,1,0:T(8,128)(2,1)S(1)} %get-tuple-element.21, f32[16,128,128]{2,1,0:T(8,128)S(1)} %fusion.22, ...), kind=kOutput, calls=%fused_computation.34 | convolution fusion | flops 405274624 | bytes 6291456 | tf_op jit(solution)/shard_map/qm,kmc->kqc/dot_general | solution.py:15
  80.3 1.2 fusion.26
  81.6 1.2 convolution_add_fusion.2
  82.8 40.1 %all-to-all-done.1 = bf16[2,2,128,1024]{2,1,0,3:T(2,128)(2,1)} async-done(((bf16[2,2,128,1024]{2,1,0,3:T(2,128)(2,1)}), bf16[2,2,128,1024]{2,1,0,3:T(2,128)(2,1)}, u32[]{:S(2)}, u32[]{:S(2)}) %all-to-all-start.1) | async-done | bytes 1048608 | tf_op jit(solution)/shard_map/all_to_all | solution.py:76
  122.9 4.3 %all-to-all-start.2 = ((bf16[128,8,128]{2,0,1:T(8,128)(2,1)}), bf16[128,8,128]{2,0,1:T(8,128)(2,1)}, u32[]{:S(2)}, u32[]{:S(2)}) async-start(bf16[128,8,128]{2,0,1:T(8,128)(2,1)} %copy.76), calls=%async_computation.2 | async-start | bytes 524288 | tf_op jit(solution)/shard_map/all_to_all | solution.py:71
  127.2 2.8 %add_bitcast_fusion.1 = (f32[16,128,128]{1,2,0:T(8,128)}, f32[16,128,128]{1,2,0:T(8,128)}) fusion(f32[16,128,128]{2,1,0:T(8,128)S(1)} %convolution_add_fusion.2, f32[16,128]{1,0:T(8,128)S(1)} %get-tuple-element.23, f32[16,128]{1,0:T(8,128)S(1)} %get-tuple-element.24, f32[16,128,128]{2,1,0:T(8,128)S(1)} %fusion.26, f32[16,128,128]{1,2,0:T(8,128)S(1)} %get-tuple-element.13), kind=kOutput, calls=%fused_computation.53 | convolution fusion | flops 404733952 | bytes 5259264 | tf_op jit(solution)/shard_map/mq,kqc->kmc/dot_general | solution.py:15
  130.0 2.6 %copy.88 = f32[16,128,128]{2,0,1:T(8,128)} copy(f32[16,128,128]{1,2,0:T(8,128)} %get-tuple-element.18) | data formatting | bytes 2097152 | tf_op jit(solution)/shard_map/sub | solution.py:49
  132.6 1.7 copy.89
  134.3 1.5 copy.129
  135.8 1.9 fusion.80
  137.7 0.0 all-to-all-done.2
  137.7 5.7 %all-to-all-start = ((bf16[128,8,128]{2,0,1:T(8,128)(2,1)}), bf16[128,8,128]{2,0,1:T(8,128)(2,1)S(1)}, u32[]{:S(2)}, u32[]{:S(2)}) async-start(bf16[128,8,128]{2,0,1:T(8,128)(2,1)} %copy.71), calls=%async_computation | async-start | bytes 524288 | tf_op jit(solution)/shard_map/all_to_all | solution.py:72
  143.4 1.9 fusion.11
  145.2 0.7 convolution_negate_fusion
  145.9 0.1 fusion.180
  146.0 1.1 fusion.178
  147.1 2.1 %fusion.18 = f32[16,128,128]{2,1,0:T(8,128)S(1)} fusion(f32[16,128,128]{2,0,1:T(8,128)S(1)} %get-tuple-element.5), kind=kOutput, calls=%fused_computation.39 | convolution fusion | flops 402882560 | bytes 2097152 | tf_op jit(solution)/shard_map/qm,kmc->kqc/dot_general | solution.py:15
  149.2 2.2 %fusion.1 = f32[16,128,128]{1,2,0:T(8,128)S(1)} fusion(f32[16,128,128]{2,1,0:T(8,128)S(1)} %fusion.18, f32[16,128,128]{2,0,1:T(8,128)S(1)} %get-tuple-element.6), kind=kOutput, calls=%fused_computation.5 | convolution fusion | flops 403177472 | bytes 3145728 | tf_op jit(solution)/shard_map/qm,kmc->kqc/dot_general | solution.py:15
  151.4 2.4 %fusion.15 = (f32[16,128,128]{1,2,0:T(8,128)S(1)}, f32[16,128,128]{1,2,0:T(8,128)S(1)}) fusion(f32[16,128,128]{1,2,0:T(8,128)S(1)} %fusion.1, bf16[1,8,2,128,128]{3,4,2,1,0:T(8,128)(2,1)S(1)} %get-tuple-element.20, bf16[1,8,2,128,128]{3,4,2,1,0:T(8,128)(2,1)S(1)} %get-tuple-element.19, f32[16,128,128]{2,1,0:T(8,128)S(1)} %fusion.18, ...), kind=kOutput, calls=%fused_computation.36 | convolution fusion | flops 405274624 | bytes 6291456 | tf_op jit(solution)/shard_map/qm,kmc->kqc/dot_general | solution.py:15
  153.8 1.2 fusion.24
  155.1 1.3 convolution_add_fusion
  156.3 1.7 add_bitcast_fusion
  158.0 0.0 copy-start.4
  158.0 1.4 copy.93
  159.4 0.5 copy.94
  160.0 1.9 fusion.76
  161.8 0.0 all-to-all-done
  161.8 0.0 copy-done.4
  161.8 0.8 fusion.10
  162.7 14.0 %all_to_all.88 = bf16[8,128,128]{2,1,0:T(8,128)(2,1)S(1)} all-to-all(bf16[8,128,128]{2,1,0:T(8,128)(2,1)S(1)} %copy.95), channel_id=1, replica_groups=mesh['grp'=2,'seq'=8,'mdl'=2] {'seq'}, dimensions={0} | all-to-all | bytes 524288 | tf_op jit(solution)/shard_map/all_to_all | solution.py:86
  176.7 0.2 copy.96
  176.9 2.2 %all_gather.6 = bf16[128,2048]{0,1:T(8,128)(2,1)S(1)} all-gather(bf16[128,1024]{0,1:T(8,128)(2,1)S(1)} %bitcast.132), channel_id=1, replica_groups=mesh['grp'=2,'seq'=8,'mdl'=2] {'mdl'}, dimensions={1}, use_global_device_ids=true | all-gather | bytes 786432 | tf_op jit(solution)/shard_map/all_gather | solution.py:87
  179.1 3.6 %convolution_convert_fusion = bf16[128,1024]{1,0:T(8,128)(2,1)} fusion(bf16[128,2048]{0,1:T(8,128)(2,1)S(1)} %all_gather.6, bf16[2048,1024]{1,0:T(8,128)(2,1)} %all-gather.2.cloned.1.call-done), kind=kOutput, calls=%fused_computation.32 | convolution fusion | flops 537001984 | bytes 4980736 | tf_op jit(solution)/shard_map/dot_general | solution.py:88
  (5 shorter events, 0.0 us)
Async XLA Ops:
  6.5 23.0 %copy-start.2 = (bf16[128,1024]{1,0:T(8,128)(2,1)S(1)}, bf16[128,1024]{1,0:T(8,128)(2,1)}, u32[]{:S(2)}) copy-start(bf16[128,1024]{1,0:T(8,128)(2,1)} %param.9) | copy-start | bytes 786436
  6.5 24.0 %copy-start.1 = (bf16[2,2,128,1024]{3,2,1,0:T(8,128)(2,1)S(1)}, bf16[2,2,128,1024]{3,2,1,0:T(8,128)(2,1)}, u32[]{:S(2)}) copy-start(bf16[2,2,128,1024]{3,2,1,0:T(8,128)(2,1)} %param.12) | copy-start | bytes 3145732
  8.6 26.7 %copy-start.3 = (bf16[128,1024]{1,0:T(8,128)(2,1)S(1)}, bf16[128,1024]{1,0:T(8,128)(2,1)}, u32[]{:S(2)}) copy-start(bf16[128,1024]{1,0:T(8,128)(2,1)} %param.10) | copy-start | bytes 786436
  8.6 16.3 %all-to-all-start.4 = ((bf16[128,8,128]{2,0,1:T(8,128)(2,1)}), bf16[128,8,128]{2,0,1:T(8,128)(2,1)S(1)}, u32[]{:S(2)}, u32[]{:S(2)}) async-start(bf16[128,8,128]{2,0,1:T(8,128)(2,1)} %copy.81), calls=%async_computation.4 | async-start | bytes 524288 | tf_op jit(solution)/shard_map/all_to_all | solution.py:70
  24.9 43.9 %all-to-all-start.3 = ((bf16[2,2,128,1024]{2,1,0,3:T(2,128)(2,1)}), bf16[2,2,128,1024]{2,1,0,3:T(2,128)(2,1)S(1)}, u32[]{:S(2)}, u32[]{:S(2)}) async-start(bf16[2,2,128,1024]{2,1,0,3:T(2,128)(2,1)} %copy.78), calls=%async_computation.3 | async-start | bytes 2097152 | tf_op jit(solution)/shard_map/all_to_all | solution.py:75
  28.5 150.6 %all-gather.2.cloned.1.call-start = ((), (), s32[]{:S(2)}) async-start(), calls=%async_computation.6 | async-start | bytes 4718592 | tf_op jit(solution)/shard_map/all_gather | solution.py:90
  68.8 54.1 %all-to-all-start.1 = ((bf16[2,2,128,1024]{2,1,0,3:T(2,128)(2,1)}), bf16[2,2,128,1024]{2,1,0,3:T(2,128)(2,1)}, u32[]{:S(2)}, u32[]{:S(2)}) async-start(bf16[2,2,128,1024]{2,1,0,3:T(2,128)(2,1)} %copy.73), calls=%async_computation.1 | async-start | bytes 2097152 | tf_op jit(solution)/shard_map/all_to_all | solution.py:76
  75.4 2.5 %copy-start = (f32[16,128,128]{2,0,1:T(8,128)S(1)}, f32[16,128,128]{2,0,1:T(8,128)}, u32[]{:S(2)}) copy-start(f32[16,128,128]{2,0,1:T(8,128)} %get-tuple-element.10) | copy-start | bytes 3145732
  122.9 14.7 %all-to-all-start.2 = ((bf16[128,8,128]{2,0,1:T(8,128)(2,1)}), bf16[128,8,128]{2,0,1:T(8,128)(2,1)}, u32[]{:S(2)}, u32[]{:S(2)}) async-start(bf16[128,8,128]{2,0,1:T(8,128)(2,1)} %copy.76), calls=%async_computation.2 | async-start | bytes 524288 | tf_op jit(solution)/shard_map/all_to_all | solution.py:71
  137.7 24.2 %all-to-all-start = ((bf16[128,8,128]{2,0,1:T(8,128)(2,1)}), bf16[128,8,128]{2,0,1:T(8,128)(2,1)S(1)}, u32[]{:S(2)}, u32[]{:S(2)}) async-start(bf16[128,8,128]{2,0,1:T(8,128)(2,1)} %copy.71), calls=%async_computation | async-start | bytes 524288 | tf_op jit(solution)/shard_map/all_to_all | solution.py:72
  158.0 3.8 %copy-start.4 = (f32[128]{0:T(128)S(1)}, f32[128]{0:T(128)}, u32[]{:S(2)}) copy-start(f32[128]{0:T(128)} %dynamic_slice.7) | copy-start | bytes 1540
Sparse Core Ops, SparseCore 0:
  31.5 104.5 all-gather.1
where the time goes:
time: 191 us; the launch traced here: 190 us
  waiting for transfers between devices  75.3 us (39%)
  matrix products  37.8 us (20%)
  starting transfers between devices  25.4 us (13%)
  local copies, waits for them, and re-layouts  21.1 us (11%)
  blocking collectives  16.2 us (8%)
  between operations  13.7 us (7%)
    all_to_all x1, waiting for transfers between devices, shards(): lax.all_to_all(spectrum_second, 'seq', split_axis=3, concat_axis=1, tiled...  40.1 us
    dot_general x20, matrix products, mixing(): return jnp.einsum(form, left, right, precision=lax.Precision.HIGHEST)  34.2 us
    all_to_all x1, waiting for transfers between devices, shards(): lax.all_to_all(spectrum_first, 'seq', split_axis=3, concat_axis=1, tiled=...  29.2 us
    all_to_all x1, blocking collectives, shards(): lax.all_to_all(mixed_cols, 'seq', split_axis=0, concat_axis=1, tiled=True)  14 us
    all_to_all x1, starting transfers between devices, shards(): lax.all_to_all(signal, 'seq', split_axis=1, concat_axis=0, tiled=True)  7.38 us
    unnamed x15, local copies, waits for them, and re-layouts  7.3 us
    all_to_all x1, starting transfers between devices, shards(): lax.all_to_all(gate_second, 'seq', split_axis=1, concat_axis=0, tiled=True)  5.69 us
    all_to_all x1, waiting for transfers between devices, shards(): lax.all_to_all(signal, 'seq', split_axis=1, concat_axis=0, tiled=True)  5.23 us
  transfers between devices with their start and end apart: 6, of which 3 were waited for; matrix products, arithmetic and copies ran while one was open for 28% of the time, Pallas kernels for 0%

commit v1 on v0

--- a/solution.py
+++ b/solution.py
@@ -3,6 +3,24 @@
 import jax.numpy as jnp
 from jax import lax
 from jax.sharding import PartitionSpec as P
+
+
+def treat_the_roots(local_block, dim_k, arr_in):
+    shaped = local_block.shape
+    then = local_block.reshape(
+        *shaped[:dim_k], arr_in, shaped[dim_k] // arr_in, *shaped[dim_k + 1 :]
+    )
+    return jnp.moveaxis(then, dim_k, 0)
+
+
+def kinds_touch(packet, axis_no):
+    packet = jnp.moveaxis(packet, 0, axis_no)
+    current_value = packet.shape
+    return packet.reshape(
+        *current_value[:axis_no],
+        current_value[axis_no] * current_value[axis_no + 1],
+        *current_value[axis_no + 2 :]
+    )
 
 
 def angle_grid(first, second, modulus):
@@ -71,9 +89,26 @@
         lax.all_to_all(gate_first, "seq", split_axis=1, concat_axis=0, tiled=True),
         lax.all_to_all(gate_second, "seq", split_axis=1, concat_axis=0, tiled=True),
     )
+
+    def recast_wall_up(piece_in, axis_key, x0, message):
+        z2 = lax.axis_index(axis_key)
+        built = lax.axis_size(axis_key)
+        carry_in, far_arr = (built, z2)
+        formed = treat_the_roots(piece_in, x0, carry_in)
+        panels = [formed[far_arr]]
+        for i0 in tuple(range(1, carry_in)):
+            res = formed[far_arr ^ i0]
+            carry = lax.ppermute(
+                res, axis_name=axis_key, perm=[(c, c ^ i0) for c in range(carry_in)]
+            )
+            panels.append(carry)
+        u1 = jnp.stack(panels, 0)
+        formed = u1[far_arr ^ jnp.arange(carry_in)]
+        return kinds_touch(formed, message)
+
     spec_one, spec_two = (
         lax.all_to_all(spectrum_first, "seq", split_axis=3, concat_axis=1, tiled=True),
-        lax.all_to_all(spectrum_second, "seq", split_axis=3, concat_axis=1, tiled=True),
+        recast_wall_up(spectrum_second, "seq", 3, 1),
     )
     skip_one = lax.dynamic_slice_in_dim(skip_first, seq_index * cols, cols, 0)
     skip_two = lax.dynamic_slice_in_dim(skip_second, seq_index * cols, cols, 0)

time: 191 us -> 167 us (0.87)
  waiting for transfers between devices: 75.3 us -> 31.1 us
  starting transfers between devices: 25.4 us -> 34.5 us
  local copies, waits for them, and re-layouts: 21.1 us -> 28.8 us
  other arithmetic: 0.06 us -> 2.58 us
    all_to_all x1 -> x0, waiting for transfers between devices: 40.1 us -> none  [shards(): lax.all_to_all(spectrum_second, 'seq', split_axis=3, concat_axis=1, tiled...]
    ppermute x0 -> x7, starting transfers between devices: none -> 11.3 us  [recast_wall_up(): lax.ppermute(res, axis_name=axis_key, perm=[(c, c ^ i0) for c in range(ca...]
    all_to_all x1, waiting for transfers between devices: 5.23 us -> 0.01 us  [shards(): lax.all_to_all(signal, 'seq', split_axis=1, concat_axis=0, tiled=True)]
    all_to_all x1 -> x0, starting transfers between devices: 4.43 us -> none  [shards(): lax.all_to_all(spectrum_second, 'seq', split_axis=3, concat_axis=1, tiled...]
    another operation x0 -> x10, local copies, waits for them, and re-layouts: none -> 3.8 us
    ppermute x0 -> x7, waiting for transfers between devices: none -> 3.09 us  [recast_wall_up(): lax.ppermute(res, axis_name=axis_key, perm=[(c, c ^ i0) for c in range(ca...]
    unnamed x15 -> x24, local copies, waits for them, and re-layouts: 7.3 us -> 10.1 us
    all_to_all x1, starting transfers between devices: 3.59 us -> 5.94 us  [shards(): lax.all_to_all(spectrum_first, 'seq', split_axis=3, concat_axis=1, tiled=...]
  transfers between devices with their start and end apart: 6 -> 12, of which waited for: 3 -> 3; matrix products, arithmetic and copies ran while one was open for 28% -> 39% of each run, Pallas kernels for 0% -> 0%
where the time goes in v1:
time: 167 us; the launch traced here: 166 us
  matrix products  38.6 us (23%)
  starting transfers between devices  34.5 us (21%)
  waiting for transfers between devices  31.1 us (19%)
  local copies, waits for them, and re-layouts  28.8 us (17%)
  blocking collectives  16.2 us (10%)
  between operations  13.9 us (8%)
  other arithmetic  2.58 us (2%)
    dot_general x20, matrix products, mixing(): return jnp.einsum(form, left, right, precision=lax.Precision.HIGHEST)  34.9 us
    all_to_all x1, waiting for transfers between devices, shards(): lax.all_to_all(spectrum_first, 'seq', split_axis=3, concat_axis=1, tiled=...  27 us
    all_to_all x1, blocking collectives, shards(): lax.all_to_all(mixed_cols, 'seq', split_axis=0, concat_axis=1, tiled=True)  14 us
    ppermute x7, starting transfers between devices, recast_wall_up(): lax.ppermute(res, axis_name=axis_key, perm=[(c, c ^ i0) for c in range(ca...  11.3 us
    unnamed x24, local copies, waits for them, and re-layouts  10.1 us
    all_to_all x1, starting transfers between devices, shards(): lax.all_to_all(signal, 'seq', split_axis=1, concat_axis=0, tiled=True)  7.25 us
    all_to_all x1, starting transfers between devices, shards(): lax.all_to_all(spectrum_first, 'seq', split_axis=3, concat_axis=1, tiled=...  5.94 us
    all_to_all x1, starting transfers between devices, shards(): lax.all_to_all(gate_second, 'seq', split_axis=1, concat_axis=0, tiled=True)  5.03 us
  transfers between devices with their start and end apart: 12, of which 3 were waited for; matrix products, arithmetic and copies ran while one was open for 39% of the time, Pallas kernels for 0%

profile of v1, /device:TPU:0, one launch (start us, length us, event | category | flops | bytes accessed | tf_op | source)
XLA Modules:
  0.0 165.7 jit_solution(2838424728027881409)
XLA Ops:
  6.5 1.2 copy.144
  7.7 0.9 copy.145
  8.6 7.3 %all-to-all-start.3 = ((bf16[128,8,128]{2,0,1:T(8,128)(2,1)}), bf16[128,8,128]{2,0,1:T(8,128)(2,1)S(1)}, u32[]{:S(2)}, u32[]{:S(2)}) async-start(bf16[128,8,128]{2,0,1:T(8,128)(2,1)} %copy.145), calls=%async_computation.3 | async-start | bytes 524288 | tf_op jit(solution)/shard_map/all_to_all | solution.py:88
  15.9 1.6 copy.129
  17.6 0.8 constant_dynamic-slice_fusion
  18.4 0.8 copy.131
  19.2 1.9 %collective-permute-start = (bf16[2,2,128,128]{3,2,1,0:T(8,128)(2,1)}, bf16[2,2,128,128]{3,2,1,0:T(8,128)(2,1)}, u32[]{:S(2)}, u32[]{:S(2)}) collective-permute-start(bf16[2,2,128,128]{3,2,1,0:T(8,128)(2,1)} %bitcast.5), channel_id=1, source_target_pairs={{0,2},{2,0},{4,6},{6,4},{8,10},{10,8},{12,14},{14,12},{1,3},{3,1},... | collective-permute-start | bytes 393224 | tf_op jit(solution)/shard_map/ppermute | solution.py:101
  21.1 0.8 copy.132
  21.9 1.5 collective-permute-start.1
  23.4 0.8 copy.133
  24.4 2.9 %collective-permute-start.3 = (bf16[2,2,128,128]{3,2,1,0:T(8,128)(2,1)S(1)}, bf16[2,2,128,128]{3,2,1,0:T(8,128)(2,1)S(1)}, u32[]{:S(2)}, u32[]{:S(2)}) collective-permute-start(bf16[2,2,128,128]{3,2,1,0:T(8,128)(2,1)S(1)} %bitcast.166), channel_id=1, source_target_pairs={{0,8},{2,10},{4,12},{6,14},{8,0},{10,2},{12,4},{14,6},{1,9},{3,11}... | collective-permute-start | bytes 393224 | tf_op jit(solution)/shard_map/ppermute | solution.py:101
  27.4 1.5 collective-permute-start.4
  29.2 0.6 fusion.118
  30.0 2.1 %copy.142 = bf16[2,2,128,1024]{2,1,0,3:T(2,128)(2,1)} copy(bf16[2,2,128,1024]{3,2,1,0:T(8,128)(2,1)S(1)} %copy-done.2) | data formatting | bytes 2097152 | tf_op args[3]
  32.0 1.1 copy.139
  33.1 0.8 copy.140
  34.3 1.3 dynamic_slice.7
  35.5 1.3 dynamic_slice.8
  36.9 1.1 copy.126
  38.0 0.9 copy.127
  38.9 0.7 pad_clamp_fusion
  39.6 3.3 %collective-permute-start.5 = (bf16[2,2,128,128]{3,2,1,0:T(8,128)(2,1)S(1)}, bf16[2,2,128,128]{3,2,1,0:T(8,128)(2,1)S(1)}, u32[]{:S(2)}, u32[]{:S(2)}) collective-permute-start(bf16[2,2,128,128]{3,2,1,0:T(8,128)(2,1)S(1)} %bitcast.168), channel_id=1, source_target_pairs={{0,12},{2,14},{4,8},{6,10},{8,4},{10,6},{12,0},{14,2},{1,13},{3,15... | collective-permute-start | bytes 393224 | tf_op jit(solution)/shard_map/ppermute | solution.py:101
  42.8 0.9 bitcast_dynamic-update-slice_fusion.6
  43.9 0.9 bitcast_dynamic-update-slice_fusion.5
  44.8 0.9 bitcast_dynamic-update-slice_fusion.4
  45.9 5.9 %all-to-all-start.2 = ((bf16[2,2,128,1024]{2,1,0,3:T(2,128)(2,1)}), bf16[2,2,128,1024]{2,1,0,3:T(2,128)(2,1)}, u32[]{:S(2)}, u32[]{:S(2)}) async-start(bf16[2,2,128,1024]{2,1,0,3:T(2,128)(2,1)} %copy.142), calls=%async_computation.2 | async-start | bytes 2097152 | tf_op jit(solution)/shard_map/all_to_all | solution.py:110
  51.8 3.1 %collective-permute-done.6 = bf16[2,2,128,128]{3,2,1,0:T(8,128)(2,1)S(1)} collective-permute-done((bf16[2,2,128,128]{3,2,1,0:T(8,128)(2,1)S(1)}, bf16[2,2,128,128]{3,2,1,0:T(8,128)(2,1)S(1)}, u32[]{:S(2)}, u32[]{:S(2)}) %collective-permute-start.6) | collective-permute-done | bytes 131104 | tf_op jit(solution)/shard_map/ppermute | solution.py:101
  54.9 0.7 gather_fusion
  55.7 1.2 slice_convert_fusion.1
  56.9 0.3 copy.138
  57.3 1.6 copy.156
  58.8 0.7 convolution_negate_fusion.1
  59.5 2.6 %fusion.180 = (f32[16,128,128]{2,0,1:T(8,128)S(1)}, f32[16,128,128]{2,0,1:T(8,128)S(1)}, f32[16,128,128]{2,0,1:T(8,128)}) fusion(f32[16,128]{0,1:T(8,128)S(1)} %copy.148, f32[16,128,128]{2,0,1:T(8,128)S(1)} %convolution_negate_fusion.1, f32[16,128]{0,1:T(8,128)S(1)} %copy.147, bf16[128,8,128]{2,0,1:T(8,128)(2,1)S(1)} %all-to-all-done.3), kind=kOutput, calls=%fused_computation.226 | convolution fusion | flops 27002624 | bytes 4472832 | tf_op jit(solution)/shard_map/ka,amc->kmc/dot_general | solution.py:33
  62.1 2.1 %fusion.22 = f32[16,128,128]{2,1,0:T(8,128)S(1)} fusion(f32[16,128,128]{2,0,1:T(8,128)S(1)} %get-tuple-element.8), kind=kOutput, calls=%fused_computation.44 | convolution fusion | flops 402882560 | bytes 2097152 | tf_op jit(solution)/shard_map/qm,kmc->kqc/dot_general | solution.py:33
  64.2 3.2 %fusion.3 = f32[16,128,128]{1,2,0:T(8,128)} fusion(f32[16,128,128]{2,1,0:T(8,128)S(1)} %fusion.22, f32[16,128,128]{2,0,1:T(8,128)S(1)} %get-tuple-element.9), kind=kOutput, calls=%fused_computation.13 | convolution fusion | flops 403177472 | bytes 3145728 | tf_op jit(solution)/shard_map/qm,kmc->kqc/dot_general | solution.py:33
  67.4 27.0 %all-to-all-done.2 = bf16[2,2,128,1024]{2,1,0,3:T(2,128)(2,1)} async-done(((bf16[2,2,128,1024]{2,1,0,3:T(2,128)(2,1)}), bf16[2,2,128,1024]{2,1,0,3:T(2,128)(2,1)}, u32[]{:S(2)}, u32[]{:S(2)}) %all-to-all-start.2) | async-done | bytes 1048608 | tf_op jit(solution)/shard_map/all_to_all | solution.py:110
  94.5 4.9 %all-to-all-start.1 = ((bf16[128,8,128]{2,0,1:T(8,128)(2,1)}), bf16[128,8,128]{2,0,1:T(8,128)(2,1)}, u32[]{:S(2)}, u32[]{:S(2)}) async-start(bf16[128,8,128]{2,0,1:T(8,128)(2,1)} %copy.140), calls=%async_computation.1 | async-start | bytes 524288 | tf_op jit(solution)/shard_map/all_to_all | solution.py:89
  99.4 1.6 copy.192
  101.2 2.4 %fusion.13 = (f32[16,128,128]{1,2,0:T(8,128)S(1)}, f32[16,128,128]{1,2,0:T(8,128)S(1)}) fusion(f32[16,128,128]{1,2,0:T(8,128)S(1)} %copy-done, bf16[1,8,2,128,128]{3,4,2,1,0:T(8,128)(2,1)S(1)} %get-tuple-element.30, bf16[1,8,2,128,128]{3,4,2,1,0:T(8,128)(2,1)S(1)} %get-tuple-element.29, f32[16,128,128]{2,1,0:T(8,128)S(1)} %fusion.22, ...), kind=kOutput, calls=%fused_computation.31 | convolution fusion | flops 405274624 | bytes 6291456 | tf_op jit(solution)/shard_map/qm,kmc->kqc/dot_general | solution.py:33
  103.6 1.2 fusion.26
  104.8 1.3 convolution_add_fusion.2
  106.1 2.4 %add_bitcast_fusion.1 = (f32[16,128,128]{1,2,0:T(8,128)S(1)}, f32[16,128,128]{1,2,0:T(8,128)}) fusion(f32[16,128,128]{2,1,0:T(8,128)S(1)} %convolution_add_fusion.2, f32[16,128]{1,0:T(8,128)S(1)} %get-tuple-element.31, f32[16,128]{1,0:T(8,128)S(1)} %get-tuple-element.32, f32[16,128,128]{2,1,0:T(8,128)S(1)} %fusion.26, f32[16,128,128]{1,2,0:T(8,128)S(1)} %get-tuple-element.13), kind=kOutput, calls=%fused_computation.53 | convolution fusion | flops 404733952 | bytes 5259264 | tf_op jit(solution)/shard_map/mq,kqc->kmc/dot_general | solution.py:33
  108.5 2.6 %copy.152 = f32[16,128,128]{2,0,1:T(8,128)} copy(f32[16,128,128]{1,2,0:T(8,128)} %get-tuple-element.18) | data formatting | bytes 2097152 | tf_op jit(solution)/shard_map/sub | solution.py:67
  111.1 1.4 copy.153
  112.5 1.9 %fusion.80 = f32[8,128,128]{2,0,1:T(8,128)S(1)} fusion(f32[16,128,128]{2,0,1:T(8,128)} %copy.152), kind=kOutput, calls=%fused_computation.125 | convolution fusion | flops 25167616 | bytes 1572864 | tf_op jit(solution)/shard_map/ka,kmc->amc/dot_general | solution.py:33
  114.4 1.0 all-to-all-done.1
  115.4 5.0 %all-to-all-start = ((bf16[128,8,128]{2,0,1:T(8,128)(2,1)}), bf16[128,8,128]{2,0,1:T(8,128)(2,1)}, u32[]{:S(2)}, u32[]{:S(2)}) async-start(bf16[128,8,128]{2,0,1:T(8,128)(2,1)} %copy.127), calls=%async_computation | async-start | bytes 524288 | tf_op jit(solution)/shard_map/all_to_all | solution.py:90
  120.4 2.2 %fusion.11 = bf16[8,128,128]{2,0,1:T(8,128)(2,1)S(1)} fusion(f32[8,128,128]{2,0,1:T(8,128)S(1)} %fusion.80, f32[16,128,128]{2,0,1:T(8,128)} %copy.153, bf16[128,8,128]{2,0,1:T(8,128)(2,1)} %all-to-all-done.1, f32[128]{0:T(128)} %dynamic_slice.7, bf16[128,8,128]{2,0,1:T(8,128)(2,1)S(1)} %all-to-all-done.3), kind=kOutput, calls=%fused_computation.28 | convolution fusion | flops 26216192 | bytes 2359808 | tf_op jit(solution)/shard_map/ka,kmc->amc/dot_general | solution.py:33
  122.7 0.7 convolution_negate_fusion
  123.4 1.1 fusion.179
  124.4 2.1 %fusion.18 = f32[16,128,128]{2,1,0:T(8,128)S(1)} fusion(f32[16,128,128]{2,0,1:T(8,128)S(1)} %get-tuple-element.5), kind=kOutput, calls=%fused_computation.40 | convolution fusion | flops 402882560 | bytes 2097152 | tf_op jit(solution)/shard_map/qm,kmc->kqc/dot_general | solution.py:33
  126.6 2.2 %fusion = f32[16,128,128]{1,2,0:T(8,128)S(1)} fusion(f32[16,128,128]{2,1,0:T(8,128)S(1)} %fusion.18, f32[16,128,128]{2,0,1:T(8,128)S(1)} %get-tuple-element.7), kind=kOutput, calls=%fused_computation.4 | convolution fusion | flops 403177472 | bytes 3145728 | tf_op jit(solution)/shard_map/qm,kmc->kqc/dot_general | solution.py:33
  128.8 2.3 %fusion.15 = (f32[16,128,128]{1,2,0:T(8,128)S(1)}, f32[16,128,128]{1,2,0:T(8,128)S(1)}) fusion(f32[1,8,2,128,128]{3,4,2,1,0:T(8,128)S(1)} %copy.156, f32[16,128,128]{1,2,0:T(8,128)S(1)} %fusion, f32[1,8,2,128,128]{3,4,2,1,0:T(8,128)S(1)} %copy.138, f32[16,128,128]{2,1,0:T(8,128)S(1)} %fusion.18, f32[16,128,128]{2,0,1:T(8,128)S(1)} %get-tuple-element.6), kind=kOutput, calls=%fused_computation.35 | convolution fusion | flops 404750336 | bytes 7340032 | tf_op jit(solution)/shard_map/qm,kmc->kqc/dot_general | solution.py:33
  131.1 1.2 fusion.24
  132.3 1.3 convolution_add_fusion
  133.6 1.7 %add_bitcast_fusion = (f32[16,128,128]{1,2,0:T(8,128)S(1)}, f32[16,128,128]{1,2,0:T(8,128)S(1)}) fusion(f32[16,128,128]{2,1,0:T(8,128)S(1)} %convolution_add_fusion, f32[16,128]{1,0:T(8,128)S(1)} %get-tuple-element.31, f32[16,128]{1,0:T(8,128)S(1)} %get-tuple-element.32, f32[16,128,128]{2,1,0:T(8,128)S(1)} %fusion.24, f32[16,128,128]{1,2,0:T(8,128)S(1)} %get-tuple-element.11), kind=kOutput, calls=%fused_computation.47 | convolution fusion | flops 404733952 | bytes 5259264 | tf_op jit(solution)/shard_map/mq,kqc->kmc/dot_general | solution.py:33
  135.3 0.5 copy.158
  135.8 0.5 copy.159
  136.3 0.6 fusion.76
  137.0 1.7 %fusion.10 = bf16[8,128,128]{2,0,1:T(8,128)(2,1)S(1)} fusion(f32[8,128,128]{2,0,1:T(8,128)S(1)} %fusion.76, f32[16,128,128]{2,0,1:T(8,128)S(1)} %copy.159, bf16[8,128,128]{2,0,1:T(8,128)(2,1)S(1)} %fusion.11, bf16[128,8,128]{2,0,1:T(8,128)(2,1)} %all-to-all-done, f32[128]{0:T(128)S(1)} %copy-done.5), kind=kOutput, calls=%fused_computation.27 | convolution fusion | flops 26216192 | bytes 2359808 | tf_op jit(solution)/shard_map/ka,kmc->amc/dot_general | solution.py:33
  138.8 14.0 %all_to_all.73 = bf16[8,128,128]{2,1,0:T(8,128)(2,1)S(1)} all-to-all(bf16[8,128,128]{2,1,0:T(8,128)(2,1)S(1)} %copy.160), channel_id=1, replica_groups=mesh['grp'=2,'seq'=8,'mdl'=2] {'seq'}, dimensions={0} | all-to-all | bytes 524288 | tf_op jit(solution)/shard_map/all_to_all | solution.py:121
  152.8 0.2 copy.161
  153.0 2.2 %all_gather.6 = bf16[128,2048]{0,1:T(8,128)(2,1)S(1)} all-gather(bf16[128,1024]{0,1:T(8,128)(2,1)S(1)} %bitcast.161), channel_id=1, replica_groups=mesh['grp'=2,'seq'=8,'mdl'=2] {'mdl'}, dimensions={1}, use_global_device_ids=true | all-gather | bytes 786432 | tf_op jit(solution)/shard_map/all_gather | solution.py:122
  155.2 3.6 %convolution_convert_fusion = bf16[128,1024]{1,0:T(8,128)(2,1)} fusion(bf16[128,2048]{0,1:T(8,128)(2,1)S(1)} %all_gather.6, bf16[2048,1024]{1,0:T(8,128)(2,1)} %all-gather.2.cloned.1.call-done), kind=kOutput, calls=%fused_computation.29 | convolution fusion | flops 537001984 | bytes 4980736 | tf_op jit(solution)/shard_map/dot_general | solution.py:123
  (40 shorter events, 1.6 us)
Async XLA Ops:
  6.5 23.4 %copy-start.2 = (bf16[2,2,128,1024]{3,2,1,0:T(8,128)(2,1)S(1)}, bf16[2,2,128,1024]{3,2,1,0:T(8,128)(2,1)}, u32[]{:S(2)}) copy-start(bf16[2,2,128,1024]{3,2,1,0:T(8,128)(2,1)} %param.11) | copy-start | bytes 3145732
  8.6 37.2 %all-to-all-start.3 = ((bf16[128,8,128]{2,0,1:T(8,128)(2,1)}), bf16[128,8,128]{2,0,1:T(8,128)(2,1)S(1)}, u32[]{:S(2)}, u32[]{:S(2)}) async-start(bf16[128,8,128]{2,0,1:T(8,128)(2,1)} %copy.145), calls=%async_computation.3 | async-start | bytes 524288 | tf_op jit(solution)/shard_map/all_to_all | solution.py:88
  15.9 139.3 %all-gather.2.cloned.1.call-start = ((), (), s32[]{:S(2)}) async-start(), calls=%async_computation.5 | async-start | bytes 4718592 | tf_op jit(solution)/shard_map/all_gather | solution.py:125
  18.4 15.6 %copy-start.4 = (bf16[2,2,128,1,128]{2,4,3,1,0:T(8,128)(2,1)S(1)}, bf16[2,2,128,1,128]{2,4,3,1,0:T(8,128)(2,1)}, u32[]{:S(2)}) copy-start(bf16[2,2,128,1,128]{2,4,3,1,0:T(8,128)(2,1)} %get-tuple-element.22) | copy-start | bytes 393220
  18.4 15.7 %copy-start.3 = (bf16[2,2,128,1,128]{2,4,3,1,0:T(8,128)(2,1)S(1)}, bf16[2,2,128,1,128]{2,4,3,1,0:T(8,128)(2,1)}, u32[]{:S(2)}) copy-start(bf16[2,2,128,1,128]{2,4,3,1,0:T(8,128)(2,1)} %get-tuple-element.21) | copy-start | bytes 393220
  19.2 20.4 %collective-permute-start = (bf16[2,2,128,128]{3,2,1,0:T(8,128)(2,1)}, bf16[2,2,128,128]{3,2,1,0:T(8,128)(2,1)}, u32[]{:S(2)}, u32[]{:S(2)}) collective-permute-start(bf16[2,2,128,128]{3,2,1,0:T(8,128)(2,1)} %bitcast.5), channel_id=1, source_target_pairs={{0,2},{2,0},{4,6},{6,4},{8,10},{10,8},{12,14},{14,12},{1,3},{3,1},... | collective-permute-start | bytes 393224 | tf_op jit(solution)/shard_map/ppermute | solution.py:101
  21.9 21.9 %collective-permute-start.1 = (bf16[2,2,128,128]{3,2,1,0:T(8,128)(2,1)}, bf16[2,2,128,128]{3,2,1,0:T(8,128)(2,1)}, u32[]{:S(2)}, u32[]{:S(2)}) collective-permute-start(bf16[2,2,128,128]{3,2,1,0:T(8,128)(2,1)} %bitcast.7), channel_id=1, source_target_pairs={{0,4},{2,6},{4,0},{6,2},{8,12},{10,14},{12,8},{14,10},{1,5},{3,7},... | collective-permute-start | bytes 393224 | tf_op jit(solution)/shard_map/ppermute | solution.py:101
  24.1 20.7 %collective-permute-start.2 = (bf16[2,2,128,128]{3,2,1,0:T(8,128)(2,1)}, bf16[2,2,128,128]{3,2,1,0:T(8,128)(2,1)}, u32[]{:S(2)}, u32[]{:S(2)}) collective-permute-start(bf16[2,2,128,128]{3,2,1,0:T(8,128)(2,1)} %bitcast.9), channel_id=1, source_target_pairs={{0,6},{2,4},{4,2},{6,0},{8,14},{10,12},{12,10},{14,8},{1,7},{3,5},... | collective-permute-start | bytes 393224 | tf_op jit(solution)/shard_map/ppermute | solution.py:101
  24.4 21.4 %collective-permute-start.3 = (bf16[2,2,128,128]{3,2,1,0:T(8,128)(2,1)S(1)}, bf16[2,2,128,128]{3,2,1,0:T(8,128)(2,1)S(1)}, u32[]{:S(2)}, u32[]{:S(2)}) collective-permute-start(bf16[2,2,128,128]{3,2,1,0:T(8,128)(2,1)S(1)} %bitcast.166), channel_id=1, source_target_pairs={{0,8},{2,10},{4,12},{6,14},{8,0},{10,2},{12,4},{14,6},{1,9},{3,11}... | collective-permute-start | bytes 393224 | tf_op jit(solution)/shard_map/ppermute | solution.py:101
  27.4 18.4 %collective-permute-start.4 = (bf16[2,2,128,128]{3,2,1,0:T(8,128)(2,1)S(1)}, bf16[2,2,128,128]{3,2,1,0:T(8,128)(2,1)S(1)}, u32[]{:S(2)}, u32[]{:S(2)}) collective-permute-start(bf16[2,2,128,128]{3,2,1,0:T(8,128)(2,1)S(1)} %bitcast.165), channel_id=1, source_target_pairs={{0,10},{2,8},{4,14},{6,12},{8,2},{10,0},{12,6},{14,4},{1,11},{3,9}... | collective-permute-start | bytes 393224 | tf_op jit(solution)/shard_map/ppermute | solution.py:101
  39.6 12.2 %collective-permute-start.5 = (bf16[2,2,128,128]{3,2,1,0:T(8,128)(2,1)S(1)}, bf16[2,2,128,128]{3,2,1,0:T(8,128)(2,1)S(1)}, u32[]{:S(2)}, u32[]{:S(2)}) collective-permute-start(bf16[2,2,128,128]{3,2,1,0:T(8,128)(2,1)S(1)} %bitcast.168), channel_id=1, source_target_pairs={{0,12},{2,14},{4,8},{6,10},{8,4},{10,6},{12,0},{14,2},{1,13},{3,15... | collective-permute-start | bytes 393224 | tf_op jit(solution)/shard_map/ppermute | solution.py:101
  43.8 11.1 %collective-permute-start.6 = (bf16[2,2,128,128]{3,2,1,0:T(8,128)(2,1)S(1)}, bf16[2,2,128,128]{3,2,1,0:T(8,128)(2,1)S(1)}, u32[]{:S(2)}, u32[]{:S(2)}) collective-permute-start(bf16[2,2,128,128]{3,2,1,0:T(8,128)(2,1)S(1)} %bitcast.167), channel_id=1, source_target_pairs={{0,14},{2,12},{4,10},{6,8},{8,6},{10,4},{12,2},{14,0},{1,15},{3,13... | collective-permute-start | bytes 393224 | tf_op jit(solution)/shard_map/ppermute | solution.py:101
  45.9 48.6 %all-to-all-start.2 = ((bf16[2,2,128,1024]{2,1,0,3:T(2,128)(2,1)}), bf16[2,2,128,1024]{2,1,0,3:T(2,128)(2,1)}, u32[]{:S(2)}, u32[]{:S(2)}) async-start(bf16[2,2,128,1024]{2,1,0,3:T(2,128)(2,1)} %copy.142), calls=%async_computation.2 | async-start | bytes 2097152 | tf_op jit(solution)/shard_map/all_to_all | solution.py:110
  94.5 20.9 %all-to-all-start.1 = ((bf16[128,8,128]{2,0,1:T(8,128)(2,1)}), bf16[128,8,128]{2,0,1:T(8,128)(2,1)}, u32[]{:S(2)}, u32[]{:S(2)}) async-start(bf16[128,8,128]{2,0,1:T(8,128)(2,1)} %copy.140), calls=%async_computation.1 | async-start | bytes 524288 | tf_op jit(solution)/shard_map/all_to_all | solution.py:89
  99.4 1.7 %copy-start = (f32[16,128,128]{1,2,0:T(8,128)S(1)}, f32[16,128,128]{1,2,0:T(8,128)}, u32[]{:S(2)}) copy-start(f32[16,128,128]{1,2,0:T(8,128)} %fusion.3) | copy-start | bytes 3145732
  99.4 1.9 %copy-start.1 = (f32[16,128,128]{2,0,1:T(8,128)S(1)}, f32[16,128,128]{2,0,1:T(8,128)}, u32[]{:S(2)}) copy-start(f32[16,128,128]{2,0,1:T(8,128)} %get-tuple-element.10) | copy-start | bytes 3145732
  115.4 21.6 %all-to-all-start = ((bf16[128,8,128]{2,0,1:T(8,128)(2,1)}), bf16[128,8,128]{2,0,1:T(8,128)(2,1)}, u32[]{:S(2)}, u32[]{:S(2)}) async-start(bf16[128,8,128]{2,0,1:T(8,128)(2,1)} %copy.127), calls=%async_computation | async-start | bytes 524288 | tf_op jit(solution)/shard_map/all_to_all | solution.py:90
  135.3 1.7 %copy-start.5 = (f32[128]{0:T(128)S(1)}, f32[128]{0:T(128)}, u32[]{:S(2)}) copy-start(f32[128]{0:T(128)} %dynamic_slice.8) | copy-start | bytes 1540
Sparse Core Ops, SparseCore 0:
  29.1 107.9 all-gather.1
